TPU v7x, 32 devices: a whole 2x2x4 slice. The times are simulated.
32 devices in a mesh: row: 8 (over z, y), col: 4 (over x, core).
Axes of the slice: x: 2, y: 2, z: 4, core: 2. Of those that a mesh axis runs over, the one named last changes fastest.
Arguments:
- left_act: bfloat16 [768, 128], P(('row', 'col')), may hold values from -540 to 540
- right_act: bfloat16 [768, 128], P(('row', 'col')), may hold values from -6 to 6
- norm_gain: float32 [128], replicated, may hold values from 0.25 to 1.75
- norm_bias: float32 [128], replicated, may hold values from -3 to 3
- w_in: bfloat16 [128, 512], replicated, may hold values from -0.5 to 0.5
- b_in: float32 [512], replicated, may hold values from -3 to 3
- w_out: bfloat16 [512, 128], replicated, may hold values from -0.25 to 0.25
- w_bins: bfloat16 [128, 64], replicated, may hold values from -0.5 to 0.5
- labels: int32 [768, 768], P('row', 'col'), may hold values from 0 to 63, as said below
Outputs:
- grad_left: float32 [768, 128], P(('row', 'col'))
- grad_right: float32 [768, 128], P('col')
- grad_w_in: float32 [128, 512], replicated
- grad_w_out: float32 [512, 128], replicated
- grad_w_bins: float32 [128, 64], replicated
Inputs may be any that keep to these rules, and one draw needn't show every extreme that they name: labels is symmetric: labels[i, j] equals labels[j, i].
All inputs are finite; a program needn't handle non-finite values.
Results may differ from a plain program's by a relative error of at most 0.00039.
Values may be sent and summed in bfloat16 or wider, within the bound.
A program may use at most 64 MiB of HBM per device.

v0:
```python
import jax
import jax.numpy as jnp
from jax import lax
from jax.sharding import PartitionSpec as P


def inner(first, second):
    return lax.dot_general(
        first, second, (((0,), (0,)), ((), ())), preferred_element_type=jnp.float32
    )


def outer(first, second):
    return lax.dot_general(
        first, second, (((1,), (1,)), ((), ())), preferred_element_type=jnp.float32
    )


def transition(left_rows, right_cols, gain, bias, w_in, b_in, w_out):
    summed = (
        left_rows.astype(jnp.float32)[:, None, :] + right_cols.astype(jnp.float32)[None, :, :]
    ).reshape(-1, left_rows.shape[1])
    center = summed - jnp.mean(summed, axis=-1, keepdims=True)
    inv_scale = lax.rsqrt(jnp.mean(center * center, axis=-1, keepdims=True) + 1e-05)
    normal_form = center * inv_scale
    normed = (normal_form * gain + bias).astype(jnp.bfloat16)
    pre_act = jnp.dot(normed, w_in, preferred_element_type=jnp.float32) + b_in
    hidden = (pre_act * jax.nn.sigmoid(pre_act)).astype(jnp.bfloat16)
    updated = (summed + jnp.dot(hidden, w_out, preferred_element_type=jnp.float32)).astype(
        jnp.bfloat16
    )
    return (normal_form, inv_scale, normed, pre_act, hidden, updated)


def pair_backward(sym, bin_labels, parts, gain, w_in, w_out, w_bins):
    normal_form, inv_scale, normed, pre_act, hidden, updated = parts
    shifted = sym - jnp.max(sym, axis=-1, keepdims=True)
    expo = jnp.exp(shifted)
    probs = expo / jnp.sum(expo, axis=-1, keepdims=True)
    onehot = (bin_labels[..., None] == lax.iota(jnp.int32, sym.shape[-1])).astype(jnp.float32)
    logit_grad = (2.0 * (probs - onehot)).reshape(-1, sym.shape[-1]).astype(jnp.bfloat16)
    grad_bins = inner(updated, logit_grad)
    upd_grad = outer(logit_grad, w_bins)
    upd_half = upd_grad.astype(jnp.bfloat16)
    grad_out = inner(hidden, upd_half)
    hid_grad = outer(upd_half, w_out)
    sigma = jax.nn.sigmoid(pre_act)
    pre_grad = (hid_grad * sigma * (1.0 + pre_act * (1.0 - sigma))).astype(jnp.bfloat16)
    grad_in = inner(normed, pre_grad)
    norm_grad = outer(pre_grad, w_in) * gain
    pair_grad = (
        inv_scale
        * (
            norm_grad
            - jnp.mean(norm_grad, axis=-1, keepdims=True)
            - normal_form * jnp.mean(norm_grad * normal_form, axis=-1, keepdims=True)
        )
        + upd_grad
    )
    return (grad_in, grad_out, grad_bins, pair_grad)


def on_device(left_act, right_act, norm_gain, norm_bias, w_in, b_in, w_out, w_bins, labels):
    tile_rows, tile_cols = labels.shape
    width = left_act.shape[1]
    stacked = jnp.stack([left_act, right_act])
    everything = lax.all_gather(stacked, ("row", "col"), axis=1, tiled=True)
    row_block = lax.dynamic_slice_in_dim(
        everything, lax.axis_index("row") * tile_rows, tile_rows, 1
    )
    column_block = lax.dynamic_slice_in_dim(
        everything, lax.axis_index("col") * tile_cols, tile_cols, 1
    )
    stride_rows = 8
    groups = tile_rows // stride_rows

    def advance(running, record):
        left_rows, right_rows, bin_labels = record
        own_parts = transition(left_rows, column_block[1], norm_gain, norm_bias, w_in, b_in, w_out)
        own_logits = jnp.dot(own_parts[5], w_bins, preferred_element_type=jnp.float32).reshape(
            stride_rows, tile_cols, -1
        )
        far_parts = transition(column_block[0], right_rows, norm_gain, norm_bias, w_in, b_in, w_out)
        far_logits = jnp.dot(far_parts[5], w_bins, preferred_element_type=jnp.float32).reshape(
            tile_cols, stride_rows, -1
        )
        sym = own_logits + jnp.transpose(far_logits, (1, 0, 2))
        grads = pair_backward(sym, bin_labels, own_parts, norm_gain, w_in, w_out, w_bins)
        pair_grad = grads[3].reshape(stride_rows, tile_cols, width)
        running = (
            running[0] + grads[0],
            running[1] + grads[1],
            running[2] + grads[2],
            running[3] + jnp.sum(pair_grad, axis=0),
        )
        return (running, jnp.sum(pair_grad, axis=1))

    start = (
        jnp.zeros((width, w_in.shape[1]), jnp.float32),
        jnp.zeros((w_in.shape[1], width), jnp.float32),
        jnp.zeros((width, w_bins.shape[1]), jnp.float32),
        jnp.zeros((tile_cols, width), jnp.float32),
    )
    records = (
        row_block[0].reshape(groups, stride_rows, width),
        row_block[1].reshape(groups, stride_rows, width),
        labels.reshape(groups, stride_rows, tile_cols),
    )
    running, left_terms = lax.scan(advance, start, records)
    grad_left = lax.psum_scatter(
        left_terms.reshape(tile_rows, width), "col", scatter_dimension=0, tiled=True
    )
    grad_right = lax.psum(running[3], "row")
    grad_in, grad_out, grad_bins = lax.psum((running[0], running[1], running[2]), ("row", "col"))
    residues = tile_rows * lax.axis_size("row")
    return (grad_left, grad_right, grad_in / residues, grad_out / residues, grad_bins / residues)


def solution(mesh):
    placed = (
        P(("row", "col"), None),
        P(("row", "col"), None),
        P(),
        P(),
        P(),
        P(),
        P(),
        P(),
        P("row", "col"),
    )
    return jax.shard_map(
        on_device,
        mesh=mesh,
        in_specs=placed,
        out_specs=(P(("row", "col"), None), P("col", None), P(), P(), P()),
        check_vma=False,
    )
```

profile of v0, /device:TPU:0, one launch (start us, length us, event | category | flops | bytes accessed | tf_op | source)
XLA Modules:
  0.0 632.4 jit_solution(9450483110087516917)
XLA Ops:
  8.8 44.3 %all_gather.3 = bf16[2,768,128]{2,1,0:T(8,128)(2,1)S(1)} all-gather(bf16[2,24,128]{2,1,0:T(8,128)(2,1)S(1)} %pad_maximum_fusion), channel_id=1, replica_groups=mesh['row'=8,'col'=4] {'row','col'}, dimensions={1}, use_global_device_ids=true | all-gather | bytes 405504 | tf_op jit(solution)/shard_map/all_gather | solution.py:67
  54.4 369.4 %while.19 = (s32[]{:T(128)}, f32[128,512]{1,0:T(8,128)}, f32[512,128]{1,0:T(8,128)S(1)}, f32[128,64]{0,1:T(8,128)}, f32[192,128]{1,0:T(8,128)}, /*index=5*/f32[1...) while((s32[]{:T(128)}, f32[128,512]{1,0:T(8,128)}, ...), condition=%wide.region_11.12_spmd.clone, body=%wide.region_0.11_spmd.clone.sunk | while | flops 1737784448 | bytes 44289180 | solution.py:109
  69.9 5.1 fusion.121
  77.1 3.5 fusion.123
  100.7 5.1 fusion.121
  107.9 3.5 fusion.123
  131.5 5.1 fusion.121
  138.7 3.5 fusion.123
  162.3 5.1 fusion.121
  169.5 3.5 fusion.123
  193.0 5.1 fusion.121
  200.3 3.5 fusion.123
  223.8 5.1 fusion.121
  231.1 3.5 fusion.123
  254.6 5.1 fusion.121
  285.4 5.1 fusion.121
  316.2 5.1 fusion.121
  346.9 5.1 fusion.121
  377.7 5.1 fusion.121
  408.5 5.1 fusion.121
  415.8 3.5 fusion.123
  425.9 37.2 %psum.31 = f32[128,64]{0,1:T(8,128)S(1)} all-reduce(f32[128,64]{0,1:T(8,128)} %get-tuple-element.95), channel_id=1, replica_groups=mesh['row'=8,'col'=4] {'row','col'}, use_global_device_ids=true, to_apply=%region_16.17 | all-reduce | flops 8192 | bytes 65536 | tf_op jit(solution)/shard_map/psum | solution.py:114
  463.7 86.6 %all-reduce.7.cloned.1.call-done = (f32[128,512]{1,0:T(8,128)}, f32[512,128]{1,0:T(8,128)}) async-done(((f32[128,512]{1,0:T(8,128)}, f32[512,128]{1,0:T(8,128)}), (f32[128,512]{1,0:T(8,128)}, f32[512,128]{1,0:T(8,128)})) %all-reduce.7.cloned.1.call-update) | async-done | bytes 524304 | tf_op jit(solution)/shard_map/psum | solution.py:114
  553.7 69.8 %all-reduce.5.cloned.1.call-done = f32[192,128]{1,0:T(8,128)} async-done(((f32[192,128]{1,0:T(8,128)}), f32[192,128]{1,0:T(8,128)}) %all-reduce.5.cloned.1.call-update) | async-done | bytes 98320 | tf_op jit(solution)/shard_map/psum | solution.py:113
  (866 shorter events, 289.2 us)
Async XLA Ops:
  8.0 542.3 %all-reduce.7.cloned.1.call-start = ((), (), s32[]{:S(2)}) async-start(), calls=%async_computation.3 | async-start | bytes 1048576 | tf_op jit(solution)/shard_map/psum | solution.py:114
  69.9 6.7 %copy-start.12 = (f32[128,64]{0,1:T(8,128)S(1)}, f32[128,64]{0,1:T(8,128)}, u32[]{:S(2)}) copy-start(f32[128,64]{0,1:T(8,128)} %get-tuple-element.372) | copy-start | bytes 98308 | tf_op jit(solution)/shard_map/while
  69.9 6.9 %copy-start.11 = (bf16[128,64]{0,1:T(8,128)(2,1)S(1)}, bf16[128,64]{0,1:T(8,128)(2,1)}, u32[]{:S(2)}) copy-start(bf16[128,64]{0,1:T(8,128)(2,1)} %get-tuple-element.400) | copy-start | bytes 49156 | tf_op jit(solution)/shard_map/while
  100.6 6.7 %copy-start.12 = (f32[128,64]{0,1:T(8,128)S(1)}, f32[128,64]{0,1:T(8,128)}, u32[]{:S(2)}) copy-start(f32[128,64]{0,1:T(8,128)} %get-tuple-element.372) | copy-start | bytes 98308 | tf_op jit(solution)/shard_map/while
  100.7 6.9 %copy-start.11 = (bf16[128,64]{0,1:T(8,128)(2,1)S(1)}, bf16[128,64]{0,1:T(8,128)(2,1)}, u32[]{:S(2)}) copy-start(bf16[128,64]{0,1:T(8,128)(2,1)} %get-tuple-element.400) | copy-start | bytes 49156 | tf_op jit(solution)/shard_map/while
  131.5 6.7 %copy-start.12 = (f32[128,64]{0,1:T(8,128)S(1)}, f32[128,64]{0,1:T(8,128)}, u32[]{:S(2)}) copy-start(f32[128,64]{0,1:T(8,128)} %get-tuple-element.372) | copy-start | bytes 98308 | tf_op jit(solution)/shard_map/while
  131.5 6.9 %copy-start.11 = (bf16[128,64]{0,1:T(8,128)(2,1)S(1)}, bf16[128,64]{0,1:T(8,128)(2,1)}, u32[]{:S(2)}) copy-start(bf16[128,64]{0,1:T(8,128)(2,1)} %get-tuple-element.400) | copy-start | bytes 49156 | tf_op jit(solution)/shard_map/while
  162.3 6.7 %copy-start.12 = (f32[128,64]{0,1:T(8,128)S(1)}, f32[128,64]{0,1:T(8,128)}, u32[]{:S(2)}) copy-start(f32[128,64]{0,1:T(8,128)} %get-tuple-element.372) | copy-start | bytes 98308 | tf_op jit(solution)/shard_map/while
  162.3 6.9 %copy-start.11 = (bf16[128,64]{0,1:T(8,128)(2,1)S(1)}, bf16[128,64]{0,1:T(8,128)(2,1)}, u32[]{:S(2)}) copy-start(bf16[128,64]{0,1:T(8,128)(2,1)} %get-tuple-element.400) | copy-start | bytes 49156 | tf_op jit(solution)/shard_map/while
  193.0 6.7 %copy-start.12 = (f32[128,64]{0,1:T(8,128)S(1)}, f32[128,64]{0,1:T(8,128)}, u32[]{:S(2)}) copy-start(f32[128,64]{0,1:T(8,128)} %get-tuple-element.372) | copy-start | bytes 98308 | tf_op jit(solution)/shard_map/while
  193.0 6.9 %copy-start.11 = (bf16[128,64]{0,1:T(8,128)(2,1)S(1)}, bf16[128,64]{0,1:T(8,128)(2,1)}, u32[]{:S(2)}) copy-start(bf16[128,64]{0,1:T(8,128)(2,1)} %get-tuple-element.400) | copy-start | bytes 49156 | tf_op jit(solution)/shard_map/while
  223.8 6.7 %copy-start.12 = (f32[128,64]{0,1:T(8,128)S(1)}, f32[128,64]{0,1:T(8,128)}, u32[]{:S(2)}) copy-start(f32[128,64]{0,1:T(8,128)} %get-tuple-element.372) | copy-start | bytes 98308 | tf_op jit(solution)/shard_map/while
  223.8 6.9 %copy-start.11 = (bf16[128,64]{0,1:T(8,128)(2,1)S(1)}, bf16[128,64]{0,1:T(8,128)(2,1)}, u32[]{:S(2)}) copy-start(bf16[128,64]{0,1:T(8,128)(2,1)} %get-tuple-element.400) | copy-start | bytes 49156 | tf_op jit(solution)/shard_map/while
  254.6 6.7 %copy-start.12 = (f32[128,64]{0,1:T(8,128)S(1)}, f32[128,64]{0,1:T(8,128)}, u32[]{:S(2)}) copy-start(f32[128,64]{0,1:T(8,128)} %get-tuple-element.372) | copy-start | bytes 98308 | tf_op jit(solution)/shard_map/while
  254.6 6.9 %copy-start.11 = (bf16[128,64]{0,1:T(8,128)(2,1)S(1)}, bf16[128,64]{0,1:T(8,128)(2,1)}, u32[]{:S(2)}) copy-start(bf16[128,64]{0,1:T(8,128)(2,1)} %get-tuple-element.400) | copy-start | bytes 49156 | tf_op jit(solution)/shard_map/while
  285.4 6.9 %copy-start.11 = (bf16[128,64]{0,1:T(8,128)(2,1)S(1)}, bf16[128,64]{0,1:T(8,128)(2,1)}, u32[]{:S(2)}) copy-start(bf16[128,64]{0,1:T(8,128)(2,1)} %get-tuple-element.400) | copy-start | bytes 49156 | tf_op jit(solution)/shard_map/while
  316.2 6.7 %copy-start.12 = (f32[128,64]{0,1:T(8,128)S(1)}, f32[128,64]{0,1:T(8,128)}, u32[]{:S(2)}) copy-start(f32[128,64]{0,1:T(8,128)} %get-tuple-element.372) | copy-start | bytes 98308 | tf_op jit(solution)/shard_map/while
  316.2 6.9 %copy-start.11 = (bf16[128,64]{0,1:T(8,128)(2,1)S(1)}, bf16[128,64]{0,1:T(8,128)(2,1)}, u32[]{:S(2)}) copy-start(bf16[128,64]{0,1:T(8,128)(2,1)} %get-tuple-element.400) | copy-start | bytes 49156 | tf_op jit(solution)/shard_map/while
  346.9 6.9 %copy-start.11 = (bf16[128,64]{0,1:T(8,128)(2,1)S(1)}, bf16[128,64]{0,1:T(8,128)(2,1)}, u32[]{:S(2)}) copy-start(bf16[128,64]{0,1:T(8,128)(2,1)} %get-tuple-element.400) | copy-start | bytes 49156 | tf_op jit(solution)/shard_map/while
  377.7 6.9 %copy-start.11 = (bf16[128,64]{0,1:T(8,128)(2,1)S(1)}, bf16[128,64]{0,1:T(8,128)(2,1)}, u32[]{:S(2)}) copy-start(bf16[128,64]{0,1:T(8,128)(2,1)} %get-tuple-element.400) | copy-start | bytes 49156 | tf_op jit(solution)/shard_map/while
  408.5 6.7 %copy-start.12 = (f32[128,64]{0,1:T(8,128)S(1)}, f32[128,64]{0,1:T(8,128)}, u32[]{:S(2)}) copy-start(f32[128,64]{0,1:T(8,128)} %get-tuple-element.372) | copy-start | bytes 98308 | tf_op jit(solution)/shard_map/while
  408.5 6.9 %copy-start.11 = (bf16[128,64]{0,1:T(8,128)(2,1)S(1)}, bf16[128,64]{0,1:T(8,128)(2,1)}, u32[]{:S(2)}) copy-start(bf16[128,64]{0,1:T(8,128)(2,1)} %get-tuple-element.400) | copy-start | bytes 49156 | tf_op jit(solution)/shard_map/while
  424.5 129.1 %reduce-scatter.4.cloned.1.call-start = ((), (), s32[]{:S(2)}) async-start(), calls=%async_computation.2 | async-start | bytes 61440
  425.1 198.3 %all-reduce.5.cloned.1.call-start = ((), (), s32[]{:S(2)}) async-start(), calls=%async_computation.1 | async-start | bytes 196608 | tf_op jit(solution)/shard_map/psum | solution.py:113
  (184 other events, 529.1 us)
Sparse Core Ops, SparseCore 0:
  424.7 125.5 all-reduce.6
  554.2 69.1 all-reduce.4
Sparse Core Ops, SparseCore 1:
  428.0 15.6 reduce-scatter.3
where the time goes:
time: 636 us; the launch traced here: 632 us
  matrix products  222 us (35%)
  waiting for transfers between devices  158 us (25%)
  local copies, waits for them, and re-layouts  85.1 us (13%)
  blocking collectives  81.5 us (13%)
  other arithmetic  65.9 us (10%)
  between operations  15.5 us (2%)
    psum x1, waiting for transfers between devices, on_device(): lax.psum((running[0], running[1], running[2]), ('row', 'col'))  86.6 us
    psum x1, waiting for transfers between devices, on_device(): grad_right = lax.psum(running[3], 'row')  69.8 us
    div x12, matrix products, pair_backward(): probs = expo / jnp.sum(expo, axis=-1, keepdims=True)  60.6 us
    dot_general x36, matrix products, outer(): lax.dot_general(first, second, (((1,), (1,)), ((), ())), preferred_elemen...  57.6 us
    dot_general x24, matrix products, transition(): jnp.dot(hidden, w_out, preferred_element_type=jnp.float32)  45.4 us
    all_gather x1, blocking collectives, on_device(): everything = lax.all_gather(stacked, ('row', 'col'), axis=1, tiled=True)  44.3 us
    psum x1, blocking collectives, on_device(): lax.psum((running[0], running[1], running[2]), ('row', 'col'))  37.2 us
    dot_general x12, matrix products, transition(): pre_act = jnp.dot(normed, w_in, preferred_element_type=jnp.float32) + b_in  30.8 us
  transfers between devices with their start and end apart: 3, of which 2 were waited for; matrix products, arithmetic and copies ran while one was open for 1% of the time, Pallas kernels for 0%

commit v1 on v0

--- a/solution.py
+++ b/solution.py
@@ -110,7 +110,7 @@
     grad_left = lax.psum_scatter(
         left_terms.reshape(tile_rows, width), "col", scatter_dimension=0, tiled=True
     )
-    grad_right = lax.psum(running[3], "row")
+    grad_right = jnp.sum(lax.all_gather(running[3], "row"), axis=0)
     grad_in, grad_out, grad_bins = lax.psum((running[0], running[1], running[2]), ("row", "col"))
     residues = tile_rows * lax.axis_size("row")
     return (grad_left, grad_right, grad_in / residues, grad_out / residues, grad_bins / residues)

time: 636 us -> 565 us (0.89)
  waiting for transfers between devices: 158 us -> 54.4 us
  blocking collectives: 81.5 us -> 114 us
    psum x1 -> x0, waiting for transfers between devices: 69.8 us -> none  [on_device(): grad_right = lax.psum(running[3], 'row')]
    psum x1, waiting for transfers between devices: 86.6 us -> 53.8 us  [on_device(): lax.psum((running[0], running[1], running[2]), ('row', 'col'))]
    all_gather x0 -> x1, blocking collectives: none -> 32.7 us  [on_device(): grad_right = jnp.sum(lax.all_gather(running[3], 'row'), axis=0)]
  transfers between devices with their start and end apart: 3 -> 2, of which waited for: 2 -> 1; matrix products, arithmetic and copies ran while one was open for 1% -> 1% of each run, Pallas kernels for 0% -> 0%
where the time goes in v1:
time: 565 us; the launch traced here: 561 us
  matrix products  222 us (39%)
  blocking collectives  114 us (20%)
  local copies, waits for them, and re-layouts  83.5 us (15%)
  other arithmetic  66.6 us (12%)
  waiting for transfers between devices  54.4 us (10%)
  between operations  15.5 us (3%)
    div x12, matrix products, pair_backward(): probs = expo / jnp.sum(expo, axis=-1, keepdims=True)  60.6 us
    dot_general x36, matrix products, outer(): lax.dot_general(first, second, (((1,), (1,)), ((), ())), preferred_elemen...  57.6 us
    psum x1, waiting for transfers between devices, on_device(): lax.psum((running[0], running[1], running[2]), ('row', 'col'))  53.8 us
    dot_general x24, matrix products, transition(): jnp.dot(hidden, w_out, preferred_element_type=jnp.float32)  45.4 us
    all_gather x1, blocking collectives, on_device(): everything = lax.all_gather(stacked, ('row', 'col'), axis=1, tiled=True)  44.3 us
    psum x1, blocking collectives, on_device(): lax.psum((running[0], running[1], running[2]), ('row', 'col'))  37.3 us
    all_gather x1, blocking collectives, on_device(): grad_right = jnp.sum(lax.all_gather(running[3], 'row'), axis=0)  32.7 us
    dot_general x12, matrix products, transition(): pre_act = jnp.dot(normed, w_in, preferred_element_type=jnp.float32) + b_in  30.8 us
  transfers between devices with their start and end apart: 2, of which 1 were waited for; matrix products, arithmetic and copies ran while one was open for 1% of the time, Pallas kernels for 0%

profile of v1, /device:TPU:0, one launch (start us, length us, event | category | flops | bytes accessed | tf_op | source)
XLA Modules:
  0.0 561.1 jit_solution(12517910260999612318)
XLA Ops:
  8.8 44.3 %all_gather.9 = bf16[2,768,128]{2,1,0:T(8,128)(2,1)S(1)} all-gather(bf16[2,24,128]{2,1,0:T(8,128)(2,1)S(1)} %pad_maximum_fusion), channel_id=1, replica_groups=mesh['row'=8,'col'=4] {'row','col'}, dimensions={1}, use_global_device_ids=true | all-gather | bytes 405504 | tf_op jit(solution)/shard_map/all_gather | solution.py:67
  54.4 369.4 %while.19 = (s32[]{:T(128)}, f32[128,512]{1,0:T(8,128)}, f32[512,128]{1,0:T(8,128)S(1)}, f32[128,64]{0,1:T(8,128)}, f32[192,128]{1,0:T(8,128)}, /*index=5*/f32[1...) while((s32[]{:T(128)}, f32[128,512]{1,0:T(8,128)}, ...), condition=%wide.region_11.12_spmd.clone, body=%wide.region_0.11_spmd.clone.sunk | while | flops 1737784448 | bytes 44289180 | solution.py:109
  69.9 5.1 fusion.121
  77.1 3.5 fusion.123
  100.7 5.1 fusion.121
  107.9 3.5 fusion.123
  131.5 5.1 fusion.121
  138.7 3.5 fusion.123
  162.3 5.1 fusion.121
  169.5 3.5 fusion.123
  193.0 5.1 fusion.121
  200.3 3.5 fusion.123
  223.8 5.1 fusion.121
  231.1 3.5 fusion.123
  254.6 5.1 fusion.121
  285.4 5.1 fusion.121
  316.2 5.1 fusion.121
  346.9 5.1 fusion.121
  377.7 5.1 fusion.121
  408.5 5.1 fusion.121
  415.8 3.5 fusion.123
  425.1 37.3 %psum.23 = f32[128,64]{0,1:T(8,128)S(1)} all-reduce(f32[128,64]{0,1:T(8,128)} %get-tuple-element.95), channel_id=1, replica_groups=mesh['row'=8,'col'=4] {'row','col'}, use_global_device_ids=true, to_apply=%region_16.17 | all-reduce | flops 8192 | bytes 65536 | tf_op jit(solution)/shard_map/psum | solution.py:114
  463.0 32.7 %all-gather = f32[1536,128]{1,0:T(8,128)S(1)} all-gather(f32[192,128]{1,0:T(8,128)} %get-tuple-element.92), channel_id=2, replica_groups=mesh['row'=8,'col'=4] {'row'}, dimensions={0}, use_global_device_ids=true | all-gather | bytes 884736 | tf_op jit(solution)/shard_map/all_gather | solution.py:113
  496.5 53.8 %all-reduce.4.cloned.1.call-done = (f32[128,512]{1,0:T(8,128)}, f32[512,128]{1,0:T(8,128)}) async-done(((f32[128,512]{1,0:T(8,128)}, f32[512,128]{1,0:T(8,128)}), (f32[128,512]{1,0:T(8,128)}, f32[512,128]{1,0:T(8,128)})) %all-reduce.4.cloned.1.call-update) | async-done | bytes 524304 | tf_op jit(solution)/shard_map/psum | solution.py:114
  (864 shorter events, 287.6 us)
Async XLA Ops:
  8.0 542.3 %all-reduce.4.cloned.1.call-start = ((), (), s32[]{:S(2)}) async-start(), calls=%async_computation.2 | async-start | bytes 1048576 | tf_op jit(solution)/shard_map/psum | solution.py:114
  69.9 6.7 %copy-start.12 = (f32[128,64]{0,1:T(8,128)S(1)}, f32[128,64]{0,1:T(8,128)}, u32[]{:S(2)}) copy-start(f32[128,64]{0,1:T(8,128)} %get-tuple-element.372) | copy-start | bytes 98308 | tf_op jit(solution)/shard_map/while
  69.9 6.9 %copy-start.11 = (bf16[128,64]{0,1:T(8,128)(2,1)S(1)}, bf16[128,64]{0,1:T(8,128)(2,1)}, u32[]{:S(2)}) copy-start(bf16[128,64]{0,1:T(8,128)(2,1)} %get-tuple-element.400) | copy-start | bytes 49156 | tf_op jit(solution)/shard_map/while
  100.6 6.7 %copy-start.12 = (f32[128,64]{0,1:T(8,128)S(1)}, f32[128,64]{0,1:T(8,128)}, u32[]{:S(2)}) copy-start(f32[128,64]{0,1:T(8,128)} %get-tuple-element.372) | copy-start | bytes 98308 | tf_op jit(solution)/shard_map/while
  100.7 6.9 %copy-start.11 = (bf16[128,64]{0,1:T(8,128)(2,1)S(1)}, bf16[128,64]{0,1:T(8,128)(2,1)}, u32[]{:S(2)}) copy-start(bf16[128,64]{0,1:T(8,128)(2,1)} %get-tuple-element.400) | copy-start | bytes 49156 | tf_op jit(solution)/shard_map/while
  131.5 6.7 %copy-start.12 = (f32[128,64]{0,1:T(8,128)S(1)}, f32[128,64]{0,1:T(8,128)}, u32[]{:S(2)}) copy-start(f32[128,64]{0,1:T(8,128)} %get-tuple-element.372) | copy-start | bytes 98308 | tf_op jit(solution)/shard_map/while
  131.5 6.9 %copy-start.11 = (bf16[128,64]{0,1:T(8,128)(2,1)S(1)}, bf16[128,64]{0,1:T(8,128)(2,1)}, u32[]{:S(2)}) copy-start(bf16[128,64]{0,1:T(8,128)(2,1)} %get-tuple-element.400) | copy-start | bytes 49156 | tf_op jit(solution)/shard_map/while
  162.3 6.7 %copy-start.12 = (f32[128,64]{0,1:T(8,128)S(1)}, f32[128,64]{0,1:T(8,128)}, u32[]{:S(2)}) copy-start(f32[128,64]{0,1:T(8,128)} %get-tuple-element.372) | copy-start | bytes 98308 | tf_op jit(solution)/shard_map/while
  162.3 6.9 %copy-start.11 = (bf16[128,64]{0,1:T(8,128)(2,1)S(1)}, bf16[128,64]{0,1:T(8,128)(2,1)}, u32[]{:S(2)}) copy-start(bf16[128,64]{0,1:T(8,128)(2,1)} %get-tuple-element.400) | copy-start | bytes 49156 | tf_op jit(solution)/shard_map/while
  193.0 6.7 %copy-start.12 = (f32[128,64]{0,1:T(8,128)S(1)}, f32[128,64]{0,1:T(8,128)}, u32[]{:S(2)}) copy-start(f32[128,64]{0,1:T(8,128)} %get-tuple-element.372) | copy-start | bytes 98308 | tf_op jit(solution)/shard_map/while
  193.0 6.9 %copy-start.11 = (bf16[128,64]{0,1:T(8,128)(2,1)S(1)}, bf16[128,64]{0,1:T(8,128)(2,1)}, u32[]{:S(2)}) copy-start(bf16[128,64]{0,1:T(8,128)(2,1)} %get-tuple-element.400) | copy-start | bytes 49156 | tf_op jit(solution)/shard_map/while
  223.8 6.7 %copy-start.12 = (f32[128,64]{0,1:T(8,128)S(1)}, f32[128,64]{0,1:T(8,128)}, u32[]{:S(2)}) copy-start(f32[128,64]{0,1:T(8,128)} %get-tuple-element.372) | copy-start | bytes 98308 | tf_op jit(solution)/shard_map/while
  223.8 6.9 %copy-start.11 = (bf16[128,64]{0,1:T(8,128)(2,1)S(1)}, bf16[128,64]{0,1:T(8,128)(2,1)}, u32[]{:S(2)}) copy-start(bf16[128,64]{0,1:T(8,128)(2,1)} %get-tuple-element.400) | copy-start | bytes 49156 | tf_op jit(solution)/shard_map/while
  254.6 6.7 %copy-start.12 = (f32[128,64]{0,1:T(8,128)S(1)}, f32[128,64]{0,1:T(8,128)}, u32[]{:S(2)}) copy-start(f32[128,64]{0,1:T(8,128)} %get-tuple-element.372) | copy-start | bytes 98308 | tf_op jit(solution)/shard_map/while
  254.6 6.9 %copy-start.11 = (bf16[128,64]{0,1:T(8,128)(2,1)S(1)}, bf16[128,64]{0,1:T(8,128)(2,1)}, u32[]{:S(2)}) copy-start(bf16[128,64]{0,1:T(8,128)(2,1)} %get-tuple-element.400) | copy-start | bytes 49156 | tf_op jit(solution)/shard_map/while
  285.4 6.7 %copy-start.12 = (f32[128,64]{0,1:T(8,128)S(1)}, f32[128,64]{0,1:T(8,128)}, u32[]{:S(2)}) copy-start(f32[128,64]{0,1:T(8,128)} %get-tuple-element.372) | copy-start | bytes 98308 | tf_op jit(solution)/shard_map/while
  285.4 6.9 %copy-start.11 = (bf16[128,64]{0,1:T(8,128)(2,1)S(1)}, bf16[128,64]{0,1:T(8,128)(2,1)}, u32[]{:S(2)}) copy-start(bf16[128,64]{0,1:T(8,128)(2,1)} %get-tuple-element.400) | copy-start | bytes 49156 | tf_op jit(solution)/shard_map/while
  316.2 6.7 %copy-start.12 = (f32[128,64]{0,1:T(8,128)S(1)}, f32[128,64]{0,1:T(8,128)}, u32[]{:S(2)}) copy-start(f32[128,64]{0,1:T(8,128)} %get-tuple-element.372) | copy-start | bytes 98308 | tf_op jit(solution)/shard_map/while
  316.2 6.9 %copy-start.11 = (bf16[128,64]{0,1:T(8,128)(2,1)S(1)}, bf16[128,64]{0,1:T(8,128)(2,1)}, u32[]{:S(2)}) copy-start(bf16[128,64]{0,1:T(8,128)(2,1)} %get-tuple-element.400) | copy-start | bytes 49156 | tf_op jit(solution)/shard_map/while
  346.9 6.9 %copy-start.11 = (bf16[128,64]{0,1:T(8,128)(2,1)S(1)}, bf16[128,64]{0,1:T(8,128)(2,1)}, u32[]{:S(2)}) copy-start(bf16[128,64]{0,1:T(8,128)(2,1)} %get-tuple-element.400) | copy-start | bytes 49156 | tf_op jit(solution)/shard_map/while
  377.7 6.9 %copy-start.11 = (bf16[128,64]{0,1:T(8,128)(2,1)S(1)}, bf16[128,64]{0,1:T(8,128)(2,1)}, u32[]{:S(2)}) copy-start(bf16[128,64]{0,1:T(8,128)(2,1)} %get-tuple-element.400) | copy-start | bytes 49156 | tf_op jit(solution)/shard_map/while
  408.5 6.7 %copy-start.12 = (f32[128,64]{0,1:T(8,128)S(1)}, f32[128,64]{0,1:T(8,128)}, u32[]{:S(2)}) copy-start(f32[128,64]{0,1:T(8,128)} %get-tuple-element.372) | copy-start | bytes 98308 | tf_op jit(solution)/shard_map/while
  408.5 6.9 %copy-start.11 = (bf16[128,64]{0,1:T(8,128)(2,1)S(1)}, bf16[128,64]{0,1:T(8,128)(2,1)}, u32[]{:S(2)}) copy-start(bf16[128,64]{0,1:T(8,128)(2,1)} %get-tuple-element.400) | copy-start | bytes 49156 | tf_op jit(solution)/shard_map/while
  424.5 129.1 %reduce-scatter.4.cloned.1.call-start = ((), (), s32[]{:S(2)}) async-start(), calls=%async_computation.1 | async-start | bytes 61440
  (183 other events, 522.4 us)
Sparse Core Ops, SparseCore 0:
  424.7 125.5 all-reduce.3
Sparse Core Ops, SparseCore 1:
  428.0 15.6 reduce-scatter.3
